TPU v7x, 128 devices: a whole 4x4x4 slice. The times are simulated.
128 devices in a mesh: vox: 8 (over y, core), fas: 16 (over z, x).
Axes of the slice: x: 4, y: 4, z: 4, core: 2. Of those that a mesh axis runs over, the one named last changes fastest.
Arguments:
- signal: float32 [128, 6144], P('vox', 'fas'), may hold values from -6 to 6
- initial_weights: float32 [524288], P('fas'), may hold values from 0.1 to 2
- coefficients: bfloat16 [32768, 4096], P(('vox', 'fas')), may hold values from 0 to 0.0234375
- block_rows: int32 [32768], P(('vox', 'fas')), may hold values from 0 to 127, as said below
- block_cols: int32 [32768], P(('vox', 'fas')), may hold values from 0 to 8191, as said below
- block_atoms: int32 [32768, 64], P(('vox', 'fas')), may hold values from 0 to 359
- block_count: int32 [128], P(('vox', 'fas')), may hold values from 64 to 256, as said below
- dictionary: bfloat16 [360, 96], replicated, may hold values from -6 to 6
Outputs:
- weights: float32 [524288], P('fas')
- residual: float32 [128, 6144], P('vox', 'fas')
Inputs may be any that keep to these rules, and one draw needn't show every extreme that they name: Block slots are stored device by device: the device with vox index i and fas index f holds slots (i * 16 + f) * 256 to (i * 16 + f + 1) * 256 - 1, and every block_rows value there lies in i * 16 to (i + 1) * 16 - 1. For the slots of the device with fas index f, every block_cols value lies in f * 512 to (f + 1) * 512 - 1. `block_count`: entry i * 16 + f is the number of live slots of the device with vox index i and fas index f, its first slots; some device has all 256 live.
All inputs are finite; a program needn't handle non-finite values.
Results may differ from a plain program's by a relative error of at most 0.0003.
Values sent between devices are 32-bit elements; how exact they have to be, the bound alone decides.
A program may use at most 128 MiB of HBM per device.

v0:
```python
import jax
import jax.numpy as jnp
from jax import lax
from jax.sharding import PartitionSpec as P

BV = 64
BF = 64
DIRS = 96
ITERS = 5


def local(
    signal,
    initial_weights,
    coefficients,
    block_rows,
    block_cols,
    block_atoms,
    block_count,
    dictionary,
):
    vox_rows = signal.shape[0]
    fas_rows = initial_weights.shape[0] // BF
    slot_total = coefficients.shape[0]
    row_width = BV * DIRS
    fas_place = lax.axis_index("fas")
    rows_local = block_rows - lax.axis_index("vox") * vox_rows
    cols_local = block_cols - fas_place * fas_rows
    live_count = block_count[0]
    atom_table = dictionary[block_atoms]
    coef_view = coefficients.reshape(slot_total, BV, BF)
    group_size = min(256, slot_total)
    group_turns = (live_count + group_size - 1) // group_size
    vox_range = jnp.arange(vox_rows, dtype=jnp.int32)
    fas_range = jnp.arange(fas_rows, dtype=jnp.int32)

    def group_pieces(first_slot):
        live_mask = (first_slot + jnp.arange(group_size, dtype=jnp.int32) < live_count).astype(
            jnp.float32
        )
        return (coef_view, atom_table, rows_local, cols_local, live_mask)

    def forward_partial(values):
        table = values.reshape(fas_rows, BF)

        def forward_accumulate(turn, running):
            coef_blk, atom_blk, rows_blk, cols_blk, live_mask = group_pieces(turn * group_size)
            scaled = coef_blk.astype(jnp.float32) * table[cols_blk][:, None, :]
            image_blk = jnp.einsum(
                "kvj,kjd->kvd",
                scaled,
                atom_blk.astype(jnp.float32),
                precision=lax.Precision.HIGHEST,
                preferred_element_type=jnp.float32,
            )
            selector = (rows_blk[:, None] == vox_range[None, :]).astype(jnp.float32) * live_mask[
                :, None
            ]
            added = jnp.dot(
                selector.T,
                image_blk.reshape(group_size, row_width),
                precision=lax.Precision.HIGHEST,
                preferred_element_type=jnp.float32,
            )
            return running + added

        start = jnp.zeros((vox_rows, row_width), jnp.float32)
        return lax.fori_loop(0, group_turns, forward_accumulate, start)

    def backward_partial(rows_view):

        def backward_accumulate(turn, running):
            coef_blk, atom_blk, rows_blk, cols_blk, live_mask = group_pieces(turn * group_size)
            gathered = rows_view[rows_blk]
            inner = jnp.einsum(
                "kvj,kvd->kjd",
                coef_blk.astype(jnp.float32),
                gathered,
                precision=lax.Precision.HIGHEST,
                preferred_element_type=jnp.float32,
            )
            contrib = jnp.sum(atom_blk.astype(jnp.float32) * inner, axis=-1)
            selector = (cols_blk[:, None] == fas_range[None, :]).astype(jnp.float32) * live_mask[
                :, None
            ]
            added = jnp.dot(
                selector.T,
                contrib,
                precision=lax.Precision.HIGHEST,
                preferred_element_type=jnp.float32,
            )
            return running + added

        start = jnp.zeros((fas_rows, BF), jnp.float32)
        running = lax.fori_loop(0, group_turns, backward_accumulate, start)
        return running.reshape(-1)

    def collect(partial_value):
        return lax.psum_scatter(partial_value, "fas", scatter_dimension=1, tiled=True)

    weights = initial_weights
    residual = collect(forward_partial(weights)) - signal
    for sweep in range(ITERS):
        whole_rows = lax.all_gather(residual, "fas", axis=1, tiled=True)
        gradient = lax.psum(backward_partial(whole_rows.reshape(vox_rows, BV, DIRS)), "vox")
        projected = jnp.where((weights > 0) | (gradient < 0), gradient, 0.0)
        image_pred = collect(forward_partial(projected))
        image_local = jnp.sum(image_pred * image_pred)
        grad_sq = lax.psum(jnp.sum(projected * projected), "fas")
        image_sq = lax.psum(image_local, ("vox", "fas"))
        step_size = grad_sq / (image_sq + 1e-06)
        weights = jnp.maximum(weights - step_size * projected, 0.0)
        residual = collect(forward_partial(weights)) - signal
    return (weights, residual)


def solution(mesh):
    placed = (
        P("vox", "fas"),
        P("fas"),
        P(("vox", "fas"), None),
        P(("vox", "fas")),
        P(("vox", "fas")),
        P(("vox", "fas"), None),
        P(("vox", "fas")),
        P(),
    )
    return jax.shard_map(
        local, mesh=mesh, in_specs=placed, out_specs=(P("fas"), P("vox", "fas")), check_vma=False
    )
```

profile of v0, /device:TPU:0, one launch (start us, length us, event | category | flops | bytes accessed | tf_op | source)
XLA Modules:
  0.0 2227.8 jit_solution(15539309578874618926)
XLA Ops:
  18.6 57.4 %gather_fusion = bf16[16384,96]{1,0:T(8,128)(2,1)} fusion(bf16[360,96]{1,0:T(8,128)(2,1)S(1)} %copy.28, s32[16384]{0:T(1024)S(1)} %broadcast_clamp_fusion), kind=kCustom, calls=%fused_computation | custom fusion | bytes 6356992 | tf_op jit(solution)/shard_map/gather | solution.py:30
  105.5 74.3 %reduce-scatter.12.cloned.1.call-done = f32[16,384]{1,0:T(8,128)} async-done(((f32[16,6144]{1,0:T(8,128)}), f32[16,384]{1,0:T(8,128)}) %reduce-scatter.12.cloned.1.call-update) | async-done | bytes 24592 | tf_op jit(solution)/shard_map/reduce_scatter | solution.py:99
  224.2 58.0 %all-reduce.6.cloned.1.call-done = f32[32768]{0:T(1024)} async-done(((f32[32768]{0:T(1024)}), f32[32768]{0:T(1024)}) %all-reduce.6.cloned.1.call-update) | async-done | bytes 131088 | tf_op jit(solution)/shard_map/psum | solution.py:105
  284.7 28.3 %while.210 = (s32[]{:T(128)}, f32[16,6144]{1,0:T(8,128)S(1)}, s32[]{:T(128)}, s32[256]{0:T(256)S(1)}, s32[]{:T(128)}, /*index=5*/bf16[256,64,64]{2,1,0:T(8,128)(...) while((s32[]{:T(128)}, f32[16,6144]{1,0:T(8,128)S(1)}, ...), condition=%wide.region_10.11_spmd.clone, body=%wide.region_9.10_spmd.clone.sunk | while | flops 1512153856 | bytes 31263864 | solution.py:68
  313.8 70.8 %reduce-scatter.14.cloned.1.call-done = f32[16,384]{1,0:T(8,128)} async-done(((f32[16,6144]{1,0:T(8,128)}), f32[16,384]{1,0:T(8,128)}) %reduce-scatter.14.cloned.1.call-update) | async-done | bytes 24592 | tf_op jit(solution)/shard_map/reduce_scatter | solution.py:99
  386.1 38.8 %psum.106 = f32[]{:T(128)} all-reduce(f32[]{:T(128)} %get-tuple-element.2460), channel_id=1, replica_groups=mesh['vox'=8,'fas'=16] {'fas'}, use_global_device_ids=true, to_apply=%region_8.9 | all-reduce | flops 1 | bytes 8 | tf_op jit(solution)/shard_map/psum | solution.py:109
  424.8 62.7 %psum.107 = f32[]{:T(128)} all-reduce(f32[]{:T(128)} %multiply_reduce_fusion.9), channel_id=1, replica_groups=mesh['vox'=8,'fas'=16] {'vox','fas'}, use_global_device_ids=true, to_apply=%region_13.14 | all-reduce | flops 1 | bytes 8 | tf_op jit(solution)/shard_map/psum | solution.py:110
  518.7 69.0 %reduce-scatter.16.cloned.1.call-done = f32[16,384]{1,0:T(8,128)} async-done(((f32[16,6144]{1,0:T(8,128)}), f32[16,384]{1,0:T(8,128)}) %reduce-scatter.16.cloned.1.call-update) | async-done | bytes 24592 | tf_op jit(solution)/shard_map/reduce_scatter | solution.py:99
  632.2 58.0 %all-reduce.8.cloned.1.call-done = f32[32768]{0:T(1024)} async-done(((f32[32768]{0:T(1024)}), f32[32768]{0:T(1024)}) %all-reduce.8.cloned.1.call-update) | async-done | bytes 131088 | tf_op jit(solution)/shard_map/psum | solution.py:105
  692.7 28.2 %while.213 = (s32[]{:T(128)}, f32[16,6144]{1,0:T(8,128)S(1)}, s32[]{:T(128)}, s32[256]{0:T(256)S(1)}, s32[]{:T(128)}, /*index=5*/bf16[256,64,64]{2,1,0:T(8,128)(...) while((s32[]{:T(128)}, f32[16,6144]{1,0:T(8,128)S(1)}, ...), condition=%wide.region_24.25_spmd.clone, body=%wide.region_23.24_spmd.clone.sunk | while | flops 1512153856 | bytes 31263864 | solution.py:68
  721.7 70.8 %reduce-scatter.18.cloned.1.call-done = f32[16,384]{1,0:T(8,128)} async-done(((f32[16,6144]{1,0:T(8,128)}), f32[16,384]{1,0:T(8,128)}) %reduce-scatter.18.cloned.1.call-update) | async-done | bytes 24592 | tf_op jit(solution)/shard_map/reduce_scatter | solution.py:99
  793.8 38.8 %psum.109 = f32[]{:T(128)} all-reduce(f32[]{:T(128)} %get-tuple-element.2458), channel_id=1, replica_groups=mesh['vox'=8,'fas'=16] {'fas'}, use_global_device_ids=true, to_apply=%region_22.23 | all-reduce | flops 1 | bytes 8 | tf_op jit(solution)/shard_map/psum | solution.py:109
  832.6 62.8 %psum.110 = f32[]{:T(128)} all-reduce(f32[]{:T(128)} %multiply_reduce_fusion.8), channel_id=1, replica_groups=mesh['vox'=8,'fas'=16] {'vox','fas'}, use_global_device_ids=true, to_apply=%region_27.28 | all-reduce | flops 1 | bytes 8 | tf_op jit(solution)/shard_map/psum | solution.py:110
  897.6 28.4 %while.214 = (s32[]{:T(128)}, f32[16,6144]{1,0:T(8,128)S(1)}, s32[]{:T(128)}, s32[256]{0:T(256)S(1)}, s32[]{:T(128)}, /*index=5*/bf16[256,64,64]{2,1,0:T(8,128)(...) while((s32[]{:T(128)}, f32[16,6144]{1,0:T(8,128)S(1)}, ...), condition=%wide.region_29.30_spmd.clone, body=%wide.region_28.29_spmd.clone.sunk | while | flops 1512153856 | bytes 31263864 | solution.py:68
  926.8 69.0 %reduce-scatter.20.cloned.1.call-done = f32[16,384]{1,0:T(8,128)} async-done(((f32[16,6144]{1,0:T(8,128)}), f32[16,384]{1,0:T(8,128)}) %reduce-scatter.20.cloned.1.call-update) | async-done | bytes 24592 | tf_op jit(solution)/shard_map/reduce_scatter | solution.py:99
  1040.3 58.0 %all-reduce.10.cloned.1.call-done = f32[32768]{0:T(1024)} async-done(((f32[32768]{0:T(1024)}), f32[32768]{0:T(1024)}) %all-reduce.10.cloned.1.call-update) | async-done | bytes 131088 | tf_op jit(solution)/shard_map/psum | solution.py:105
  1129.6 70.8 %reduce-scatter.22.cloned.1.call-done = f32[16,384]{1,0:T(8,128)} async-done(((f32[16,6144]{1,0:T(8,128)}), f32[16,384]{1,0:T(8,128)}) %reduce-scatter.22.cloned.1.call-update) | async-done | bytes 24592 | tf_op jit(solution)/shard_map/reduce_scatter | solution.py:99
  1201.9 38.8 %psum.112 = f32[]{:T(128)} all-reduce(f32[]{:T(128)} %get-tuple-element.2456), channel_id=1, replica_groups=mesh['vox'=8,'fas'=16] {'fas'}, use_global_device_ids=true, to_apply=%region_36.37 | all-reduce | flops 1 | bytes 8 | tf_op jit(solution)/shard_map/psum | solution.py:109
  1240.6 62.7 %psum.113 = f32[]{:T(128)} all-reduce(f32[]{:T(128)} %multiply_reduce_fusion.7), channel_id=1, replica_groups=mesh['vox'=8,'fas'=16] {'vox','fas'}, use_global_device_ids=true, to_apply=%region_41.42 | all-reduce | flops 1 | bytes 8 | tf_op jit(solution)/shard_map/psum | solution.py:110
  1305.6 28.3 %while.217 = (s32[]{:T(128)}, f32[16,6144]{1,0:T(8,128)S(1)}, s32[]{:T(128)}, s32[256]{0:T(256)S(1)}, s32[]{:T(128)}, /*index=5*/bf16[256,64,64]{2,1,0:T(8,128)(...) while((s32[]{:T(128)}, f32[16,6144]{1,0:T(8,128)S(1)}, ...), condition=%wide.region_43.44_spmd.clone, body=%wide.region_42.43_spmd.clone.sunk | while | flops 1512153856 | bytes 31263864 | solution.py:68
  1334.7 69.1 %reduce-scatter.24.cloned.1.call-done = f32[16,384]{1,0:T(8,128)} async-done(((f32[16,6144]{1,0:T(8,128)}), f32[16,384]{1,0:T(8,128)}) %reduce-scatter.24.cloned.1.call-update) | async-done | bytes 24592 | tf_op jit(solution)/shard_map/reduce_scatter | solution.py:99
  1448.3 57.9 %all-reduce.12.cloned.1.call-done = f32[32768]{0:T(1024)} async-done(((f32[32768]{0:T(1024)}), f32[32768]{0:T(1024)}) %all-reduce.12.cloned.1.call-update) | async-done | bytes 131088 | tf_op jit(solution)/shard_map/psum | solution.py:105
  1537.6 70.8 %reduce-scatter.26.cloned.1.call-done = f32[16,384]{1,0:T(8,128)} async-done(((f32[16,6144]{1,0:T(8,128)}), f32[16,384]{1,0:T(8,128)}) %reduce-scatter.26.cloned.1.call-update) | async-done | bytes 24592 | tf_op jit(solution)/shard_map/reduce_scatter | solution.py:99
  1609.8 38.8 %psum.115 = f32[]{:T(128)} all-reduce(f32[]{:T(128)} %get-tuple-element.2454), channel_id=1, replica_groups=mesh['vox'=8,'fas'=16] {'fas'}, use_global_device_ids=true, to_apply=%region_50.51 | all-reduce | flops 1 | bytes 8 | tf_op jit(solution)/shard_map/psum | solution.py:109
  1648.6 62.8 %psum.116 = f32[]{:T(128)} all-reduce(f32[]{:T(128)} %multiply_reduce_fusion.6), channel_id=1, replica_groups=mesh['vox'=8,'fas'=16] {'vox','fas'}, use_global_device_ids=true, to_apply=%region_55.56 | all-reduce | flops 1 | bytes 8 | tf_op jit(solution)/shard_map/psum | solution.py:110
  1713.6 28.3 %while.220 = (s32[]{:T(128)}, f32[16,6144]{1,0:T(8,128)S(1)}, s32[]{:T(128)}, s32[256]{0:T(256)S(1)}, s32[]{:T(128)}, /*index=5*/bf16[256,64,64]{2,1,0:T(8,128)(...) while((s32[]{:T(128)}, f32[16,6144]{1,0:T(8,128)S(1)}, ...), condition=%wide.region_57.58_spmd.clone, body=%wide.region_56.57_spmd.clone.sunk | while | flops 1512153856 | bytes 31263864 | solution.py:68
  1742.7 69.0 %reduce-scatter.28.cloned.1.call-done = f32[16,384]{1,0:T(8,128)} async-done(((f32[16,6144]{1,0:T(8,128)}), f32[16,384]{1,0:T(8,128)}) %reduce-scatter.28.cloned.1.call-update) | async-done | bytes 24592 | tf_op jit(solution)/shard_map/reduce_scatter | solution.py:99
  1856.2 58.0 %all-reduce.14.cloned.1.call-done = f32[32768]{0:T(1024)} async-done(((f32[32768]{0:T(1024)}), f32[32768]{0:T(1024)}) %all-reduce.14.cloned.1.call-update) | async-done | bytes 131088 | tf_op jit(solution)/shard_map/psum | solution.py:105
  1945.5 70.8 %reduce-scatter.30.cloned.1.call-done = f32[16,384]{1,0:T(8,128)} async-done(((f32[16,6144]{1,0:T(8,128)}), f32[16,384]{1,0:T(8,128)}) %reduce-scatter.30.cloned.1.call-update) | async-done | bytes 24592 | tf_op jit(solution)/shard_map/reduce_scatter | solution.py:99
  2017.8 38.8 %psum.118 = f32[]{:T(128)} all-reduce(f32[]{:T(128)} %get-tuple-element.2452), channel_id=1, replica_groups=mesh['vox'=8,'fas'=16] {'fas'}, use_global_device_ids=true, to_apply=%region_64.65 | all-reduce | flops 1 | bytes 8 | tf_op jit(solution)/shard_map/psum | solution.py:109
  2056.5 62.7 %psum.119 = f32[]{:T(128)} all-reduce(f32[]{:T(128)} %multiply_reduce_fusion.5), channel_id=1, replica_groups=mesh['vox'=8,'fas'=16] {'vox','fas'}, use_global_device_ids=true, to_apply=%region_69.70 | all-reduce | flops 1 | bytes 8 | tf_op jit(solution)/shard_map/psum | solution.py:110
  2150.5 69.0 %reduce-scatter.32.cloned.1.call-done = f32[16,384]{1,0:T(8,128)} async-done(((f32[16,6144]{1,0:T(8,128)}), f32[16,384]{1,0:T(8,128)}) %reduce-scatter.32.cloned.1.call-update) | async-done | bytes 24592 | tf_op jit(solution)/shard_map/reduce_scatter | solution.py:99
  (233 shorter events, 748.5 us)
Async XLA Ops:
  7.2 10.8 copy-start.15
  7.2 11.1 copy-start.14
  7.2 11.2 copy-start.16
  7.2 11.2 copy-start.11
  7.2 172.5 %reduce-scatter.12.cloned.1.call-start = ((), (), s32[]{:S(2)}) async-start(), calls=%async_computation.11 | async-start | bytes 417792 | tf_op jit(solution)/shard_map/reduce_scatter | solution.py:99
  18.5 58.1 %copy-start.17 = (s32[256]{0:T(256)S(1)}, s32[256]{0:T(256)}, u32[]{:S(2)}) copy-start(s32[256]{0:T(256)} %param.43) | copy-start | bytes 3076
  76.7 103.0 %copy-start.12 = (f32[16,384]{1,0:T(8,128)S(1)}, f32[16,384]{1,0:T(8,128)}, u32[]{:S(2)}) copy-start(f32[16,384]{1,0:T(8,128)} %param.40) | copy-start | bytes 73732
  104.6 0.7 copy-start.1
  105.4 176.9 %all-reduce.6.cloned.1.call-start = ((), (), s32[]{:S(2)}) async-start(), calls=%async_computation.12 | async-start | bytes 262144 | tf_op jit(solution)/shard_map/psum | solution.py:105
  224.2 160.4 %reduce-scatter.14.cloned.1.call-start = ((), (), s32[]{:S(2)}) async-start(), calls=%async_computation.13 | async-start | bytes 417792 | tf_op jit(solution)/shard_map/reduce_scatter | solution.py:99
  313.0 0.7 copy-start.2
  313.8 274.0 %reduce-scatter.16.cloned.1.call-start = ((), (), s32[]{:S(2)}) async-start(), calls=%async_computation.14 | async-start | bytes 417792 | tf_op jit(solution)/shard_map/reduce_scatter | solution.py:99
  517.9 0.7 copy-start.3
  518.7 171.6 %all-reduce.8.cloned.1.call-start = ((), (), s32[]{:S(2)}) async-start(), calls=%async_computation.15 | async-start | bytes 262144 | tf_op jit(solution)/shard_map/psum | solution.py:105
  632.2 160.2 %reduce-scatter.18.cloned.1.call-start = ((), (), s32[]{:S(2)}) async-start(), calls=%async_computation.16 | async-start | bytes 417792 | tf_op jit(solution)/shard_map/reduce_scatter | solution.py:99
  721.6 274.2 %reduce-scatter.20.cloned.1.call-start = ((), (), s32[]{:S(2)}) async-start(), calls=%async_computation.17 | async-start | bytes 417792 | tf_op jit(solution)/shard_map/reduce_scatter | solution.py:99
  926.8 171.5 %all-reduce.10.cloned.1.call-start = ((), (), s32[]{:S(2)}) async-start(), calls=%async_computation.18 | async-start | bytes 262144 | tf_op jit(solution)/shard_map/psum | solution.py:105
  1040.2 160.2 %reduce-scatter.22.cloned.1.call-start = ((), (), s32[]{:S(2)}) async-start(), calls=%async_computation.19 | async-start | bytes 417792 | tf_op jit(solution)/shard_map/reduce_scatter | solution.py:99
  1128.8 0.7 copy-start.6
  1129.6 274.2 %reduce-scatter.24.cloned.1.call-start = ((), (), s32[]{:S(2)}) async-start(), calls=%async_computation.20 | async-start | bytes 417792 | tf_op jit(solution)/shard_map/reduce_scatter | solution.py:99
  1333.9 0.7 copy-start.7
  1334.7 171.5 %all-reduce.12.cloned.1.call-start = ((), (), s32[]{:S(2)}) async-start(), calls=%async_computation.21 | async-start | bytes 262144 | tf_op jit(solution)/shard_map/psum | solution.py:105
  1448.2 160.2 %reduce-scatter.26.cloned.1.call-start = ((), (), s32[]{:S(2)}) async-start(), calls=%async_computation.22 | async-start | bytes 417792 | tf_op jit(solution)/shard_map/reduce_scatter | solution.py:99
  1536.8 0.7 copy-start.8
  1537.5 274.2 %reduce-scatter.28.cloned.1.call-start = ((), (), s32[]{:S(2)}) async-start(), calls=%async_computation.23 | async-start | bytes 417792 | tf_op jit(solution)/shard_map/reduce_scatter | solution.py:99
  1741.9 0.7 copy-start.9
  1742.7 171.5 %all-reduce.14.cloned.1.call-start = ((), (), s32[]{:S(2)}) async-start(), calls=%async_computation.24 | async-start | bytes 262144 | tf_op jit(solution)/shard_map/psum | solution.py:105
  1856.1 160.2 %reduce-scatter.30.cloned.1.call-start = ((), (), s32[]{:S(2)}) async-start(), calls=%async_computation.25 | async-start | bytes 417792 | tf_op jit(solution)/shard_map/reduce_scatter | solution.py:99
  1944.7 0.7 copy-start.10
  1945.5 274.0 %reduce-scatter.32.cloned.1.call-start = ((), (), s32[]{:S(2)}) async-start(), calls=%async_computation.26 | async-start | bytes 417792 | tf_op jit(solution)/shard_map/reduce_scatter | solution.py:99
  2120.6 0.9 copy-start.13
  2149.7 0.7 copy-start
  (2 other events, 1.5 us)
Sparse Core Ops, SparseCore 0:
  105.5 74.1 reduce-scatter.11
  224.3 57.9 all-reduce.5
  313.9 70.6 reduce-scatter.13
  518.8 68.9 reduce-scatter.15
  632.3 57.8 all-reduce.7
  721.7 70.6 reduce-scatter.17
  926.9 68.9 reduce-scatter.19
  1040.4 57.8 all-reduce.9
  1129.7 70.6 reduce-scatter.21
  1334.8 68.9 reduce-scatter.23
  1448.3 57.8 all-reduce.11
  1537.7 70.6 reduce-scatter.25
  1742.8 68.9 reduce-scatter.27
  1856.3 57.8 all-reduce.13
  1945.6 70.6 reduce-scatter.29
  2150.6 68.8 reduce-scatter.31
where the time goes:
time: 2240 us; the launch traced here: 2230 us
  waiting for transfers between devices  1060 us (47%)
  blocking collectives  625 us (28%)
  matrix products  275 us (12%)
  local copies, waits for them, and re-layouts  207 us (9%)
  other arithmetic  30.5 us (1%)
  between operations  22.5 us (1%)
    reduce_scatter x11, waiting for transfers between devices, collect(): lax.psum_scatter(partial_value, 'fas', scatter_dimension=1, tiled=True)  773 us
    psum x5, blocking collectives, local(): image_sq = lax.psum(image_local, ('vox', 'fas'))  314 us
    psum x5, waiting for transfers between devices, local(): lax.psum(backward_partial(whole_rows.reshape(vox_rows, BV, DIRS)), 'vox')  290 us
    psum x5, blocking collectives, local(): grad_sq = lax.psum(jnp.sum(projected * projected), 'fas')  194 us
    dot_general x11, matrix products, forward_accumulate(): jnp.einsum('kvj,kjd->kvd', scaled, atom_blk.astype(jnp.float32), precisio...  124 us
    all_gather x5, blocking collectives, local(): whole_rows = lax.all_gather(residual, 'fas', axis=1, tiled=True)  118 us
    dot_general x11, local copies, waits for them, and re-layouts, forward_accumulate(): jnp.einsum('kvj,kjd->kvd', scaled, atom_blk.astype(jnp.float32), precisio...  94.4 us
    dot_general x11, matrix products, forward_accumulate(): jnp.dot(selector.T, image_blk.reshape(group_size, row_width), precision=l...  81.8 us
  transfers between devices with their start and end apart: 16, of which 16 were waited for; matrix products, arithmetic and copies ran while one was open for 0% of the time, Pallas kernels for 0%

commit v1 on v0

--- a/solution.py
+++ b/solution.py
@@ -102,7 +102,9 @@
     residual = collect(forward_partial(weights)) - signal
     for sweep in range(ITERS):
         whole_rows = lax.all_gather(residual, "fas", axis=1, tiled=True)
-        gradient = lax.psum(backward_partial(whole_rows.reshape(vox_rows, BV, DIRS)), "vox")
+        gradient = jnp.sum(
+            lax.all_gather(backward_partial(whole_rows.reshape(vox_rows, BV, DIRS)), "vox"), axis=0
+        )
         projected = jnp.where((weights > 0) | (gradient < 0), gradient, 0.0)
         image_pred = collect(forward_partial(projected))
         image_local = jnp.sum(image_pred * image_pred)

time: 2240 us -> 2070 us (0.924)
  waiting for transfers between devices: 1060 us -> 888 us
    psum x5 -> x0, waiting for transfers between devices: 290 us -> none  [local(): lax.psum(backward_partial(whole_rows.reshape(vox_rows, BV, DIRS)), 'vox')]
    all_gather x0 -> x5, waiting for transfers between devices: none -> 110 us  [local(): lax.all_gather(backward_partial(whole_rows.reshape(vox_rows, BV, DIRS)),...]
where the time goes in v1:
time: 2070 us; the launch traced here: 2060 us
  waiting for transfers between devices  888 us (43%)
  blocking collectives  626 us (30%)
  matrix products  275 us (13%)
  local copies, waits for them, and re-layouts  207 us (10%)
  other arithmetic  35.9 us (2%)
  between operations  22.3 us (1%)
    reduce_scatter x11, waiting for transfers between devices, collect(): lax.psum_scatter(partial_value, 'fas', scatter_dimension=1, tiled=True)  777 us
    psum x5, blocking collectives, local(): image_sq = lax.psum(image_local, ('vox', 'fas'))  314 us
    psum x5, blocking collectives, local(): grad_sq = lax.psum(jnp.sum(projected * projected), 'fas')  194 us
    dot_general x11, matrix products, forward_accumulate(): jnp.einsum('kvj,kjd->kvd', scaled, atom_blk.astype(jnp.float32), precisio...  124 us
    all_gather x5, blocking collectives, local(): whole_rows = lax.all_gather(residual, 'fas', axis=1, tiled=True)  119 us
    all_gather x5, waiting for transfers between devices, local(): lax.all_gather(backward_partial(whole_rows.reshape(vox_rows, BV, DIRS)),...  110 us
    dot_general x11, local copies, waits for them, and re-layouts, forward_accumulate(): jnp.einsum('kvj,kjd->kvd', scaled, atom_blk.astype(jnp.float32), precisio...  94.4 us
    dot_general x11, matrix products, forward_accumulate(): jnp.dot(selector.T, image_blk.reshape(group_size, row_width), precision=l...  81.8 us
  transfers between devices with their start and end apart: 16, of which 16 were waited for; matrix products, arithmetic and copies ran while one was open for 0% of the time, Pallas kernels for 0%

profile of v1, /device:TPU:0, one launch (start us, length us, event | category | flops | bytes accessed | tf_op | source)
XLA Modules:
  0.0 2058.1 jit_solution(8206460509092669613)
XLA Ops:
  18.6 57.4 %gather_fusion = bf16[16384,96]{1,0:T(8,128)(2,1)} fusion(bf16[360,96]{1,0:T(8,128)(2,1)S(1)} %copy.63, s32[16384]{0:T(1024)S(1)} %broadcast_clamp_fusion), kind=kCustom, calls=%fused_computation | custom fusion | bytes 6356992 | tf_op jit(solution)/shard_map/gather | solution.py:30
  105.5 74.3 %reduce-scatter.12.cloned.1.call-done = f32[16,384]{1,0:T(8,128)} async-done(((f32[16,6144]{1,0:T(8,128)}), f32[16,384]{1,0:T(8,128)}) %reduce-scatter.12.cloned.1.call-update) | async-done | bytes 24592 | tf_op jit(solution)/shard_map/reduce_scatter | solution.py:99
  250.2 28.1 %while.210 = (s32[]{:T(128)}, f32[16,6144]{1,0:T(8,128)S(1)}, s32[]{:T(128)}, s32[256]{0:T(256)S(1)}, s32[]{:T(128)}, /*index=5*/bf16[256,64,64]{2,1,0:T(8,128)(...) while((s32[]{:T(128)}, f32[16,6144]{1,0:T(8,128)S(1)}, ...), condition=%wide.region_10.11_spmd.clone, body=%wide.region_9.10_spmd.clone.sunk | while | flops 1512153856 | bytes 31263864 | solution.py:68
  279.1 71.6 %reduce-scatter.14.cloned.1.call-done = f32[16,384]{1,0:T(8,128)} async-done(((f32[16,6144]{1,0:T(8,128)}), f32[16,384]{1,0:T(8,128)}) %reduce-scatter.14.cloned.1.call-update) | async-done | bytes 24592 | tf_op jit(solution)/shard_map/reduce_scatter | solution.py:99
  352.1 38.8 %psum.70 = f32[]{:T(128)} all-reduce(f32[]{:T(128)} %get-tuple-element.2548), channel_id=1, replica_groups=mesh['vox'=8,'fas'=16] {'fas'}, use_global_device_ids=true, to_apply=%region_8.9 | all-reduce | flops 1 | bytes 8 | tf_op jit(solution)/shard_map/psum | solution.py:111
  390.9 62.7 %psum.71 = f32[]{:T(128)} all-reduce(f32[]{:T(128)} %multiply_reduce_fusion.9), channel_id=1, replica_groups=mesh['vox'=8,'fas'=16] {'vox','fas'}, use_global_device_ids=true, to_apply=%region_13.14 | all-reduce | flops 1 | bytes 8 | tf_op jit(solution)/shard_map/psum | solution.py:112
  455.9 28.1 %while.211 = (s32[]{:T(128)}, f32[16,6144]{1,0:T(8,128)S(1)}, s32[]{:T(128)}, s32[256]{0:T(256)S(1)}, s32[]{:T(128)}, /*index=5*/bf16[256,64,64]{2,1,0:T(8,128)(...) while((s32[]{:T(128)}, f32[16,6144]{1,0:T(8,128)S(1)}, ...), condition=%wide.region_15.16_spmd.clone, body=%wide.region_14.15_spmd.clone.sunk | while | flops 1512153856 | bytes 31263864 | solution.py:68
  484.8 69.0 %reduce-scatter.16.cloned.1.call-done = f32[16,384]{1,0:T(8,128)} async-done(((f32[16,6144]{1,0:T(8,128)}), f32[16,384]{1,0:T(8,128)}) %reduce-scatter.16.cloned.1.call-update) | async-done | bytes 24592 | tf_op jit(solution)/shard_map/reduce_scatter | solution.py:99
  624.2 28.1 %while.213 = (s32[]{:T(128)}, f32[16,6144]{1,0:T(8,128)S(1)}, s32[]{:T(128)}, s32[256]{0:T(256)S(1)}, s32[]{:T(128)}, /*index=5*/bf16[256,64,64]{2,1,0:T(8,128)(...) while((s32[]{:T(128)}, f32[16,6144]{1,0:T(8,128)S(1)}, ...), condition=%wide.region_24.25_spmd.clone, body=%wide.region_23.24_spmd.clone.sunk | while | flops 1512153856 | bytes 31263864 | solution.py:68
  653.1 71.6 %reduce-scatter.18.cloned.1.call-done = f32[16,384]{1,0:T(8,128)} async-done(((f32[16,6144]{1,0:T(8,128)}), f32[16,384]{1,0:T(8,128)}) %reduce-scatter.18.cloned.1.call-update) | async-done | bytes 24592 | tf_op jit(solution)/shard_map/reduce_scatter | solution.py:99
  726.1 38.8 %psum.72 = f32[]{:T(128)} all-reduce(f32[]{:T(128)} %get-tuple-element.2546), channel_id=1, replica_groups=mesh['vox'=8,'fas'=16] {'fas'}, use_global_device_ids=true, to_apply=%region_22.23 | all-reduce | flops 1 | bytes 8 | tf_op jit(solution)/shard_map/psum | solution.py:111
  764.9 62.7 %psum.73 = f32[]{:T(128)} all-reduce(f32[]{:T(128)} %multiply_reduce_fusion.8), channel_id=1, replica_groups=mesh['vox'=8,'fas'=16] {'vox','fas'}, use_global_device_ids=true, to_apply=%region_27.28 | all-reduce | flops 1 | bytes 8 | tf_op jit(solution)/shard_map/psum | solution.py:112
  829.9 28.1 %while.214 = (s32[]{:T(128)}, f32[16,6144]{1,0:T(8,128)S(1)}, s32[]{:T(128)}, s32[256]{0:T(256)S(1)}, s32[]{:T(128)}, /*index=5*/bf16[256,64,64]{2,1,0:T(8,128)(...) while((s32[]{:T(128)}, f32[16,6144]{1,0:T(8,128)S(1)}, ...), condition=%wide.region_29.30_spmd.clone, body=%wide.region_28.29_spmd.clone.sunk | while | flops 1512153856 | bytes 31263864 | solution.py:68
  858.9 69.0 %reduce-scatter.20.cloned.1.call-done = f32[16,384]{1,0:T(8,128)} async-done(((f32[16,6144]{1,0:T(8,128)}), f32[16,384]{1,0:T(8,128)}) %reduce-scatter.20.cloned.1.call-update) | async-done | bytes 24592 | tf_op jit(solution)/shard_map/reduce_scatter | solution.py:99
  998.2 28.1 %while.216 = (s32[]{:T(128)}, f32[16,6144]{1,0:T(8,128)S(1)}, s32[]{:T(128)}, s32[256]{0:T(256)S(1)}, s32[]{:T(128)}, /*index=5*/bf16[256,64,64]{2,1,0:T(8,128)(...) while((s32[]{:T(128)}, f32[16,6144]{1,0:T(8,128)S(1)}, ...), condition=%wide.region_38.39_spmd.clone, body=%wide.region_37.38_spmd.clone.sunk | while | flops 1512153856 | bytes 31263864 | solution.py:68
  1027.1 71.6 %reduce-scatter.22.cloned.1.call-done = f32[16,384]{1,0:T(8,128)} async-done(((f32[16,6144]{1,0:T(8,128)}), f32[16,384]{1,0:T(8,128)}) %reduce-scatter.22.cloned.1.call-update) | async-done | bytes 24592 | tf_op jit(solution)/shard_map/reduce_scatter | solution.py:99
  1100.2 38.8 %psum.74 = f32[]{:T(128)} all-reduce(f32[]{:T(128)} %get-tuple-element.2544), channel_id=1, replica_groups=mesh['vox'=8,'fas'=16] {'fas'}, use_global_device_ids=true, to_apply=%region_36.37 | all-reduce | flops 1 | bytes 8 | tf_op jit(solution)/shard_map/psum | solution.py:111
  1138.9 62.7 %psum.75 = f32[]{:T(128)} all-reduce(f32[]{:T(128)} %multiply_reduce_fusion.7), channel_id=1, replica_groups=mesh['vox'=8,'fas'=16] {'vox','fas'}, use_global_device_ids=true, to_apply=%region_41.42 | all-reduce | flops 1 | bytes 8 | tf_op jit(solution)/shard_map/psum | solution.py:112
  1203.9 28.1 %while.217 = (s32[]{:T(128)}, f32[16,6144]{1,0:T(8,128)S(1)}, s32[]{:T(128)}, s32[256]{0:T(256)S(1)}, s32[]{:T(128)}, /*index=5*/bf16[256,64,64]{2,1,0:T(8,128)(...) while((s32[]{:T(128)}, f32[16,6144]{1,0:T(8,128)S(1)}, ...), condition=%wide.region_43.44_spmd.clone, body=%wide.region_42.43_spmd.clone.sunk | while | flops 1512153856 | bytes 31263864 | solution.py:68
  1232.9 69.0 %reduce-scatter.24.cloned.1.call-done = f32[16,384]{1,0:T(8,128)} async-done(((f32[16,6144]{1,0:T(8,128)}), f32[16,384]{1,0:T(8,128)}) %reduce-scatter.24.cloned.1.call-update) | async-done | bytes 24592 | tf_op jit(solution)/shard_map/reduce_scatter | solution.py:99
  1372.3 28.1 %while.219 = (s32[]{:T(128)}, f32[16,6144]{1,0:T(8,128)S(1)}, s32[]{:T(128)}, s32[256]{0:T(256)S(1)}, s32[]{:T(128)}, /*index=5*/bf16[256,64,64]{2,1,0:T(8,128)(...) while((s32[]{:T(128)}, f32[16,6144]{1,0:T(8,128)S(1)}, ...), condition=%wide.region_52.53_spmd.clone, body=%wide.region_51.52_spmd.clone.sunk | while | flops 1512153856 | bytes 31263864 | solution.py:68
  1401.2 71.6 %reduce-scatter.26.cloned.1.call-done = f32[16,384]{1,0:T(8,128)} async-done(((f32[16,6144]{1,0:T(8,128)}), f32[16,384]{1,0:T(8,128)}) %reduce-scatter.26.cloned.1.call-update) | async-done | bytes 24592 | tf_op jit(solution)/shard_map/reduce_scatter | solution.py:99
  1474.2 38.8 %psum.76 = f32[]{:T(128)} all-reduce(f32[]{:T(128)} %get-tuple-element.2542), channel_id=1, replica_groups=mesh['vox'=8,'fas'=16] {'fas'}, use_global_device_ids=true, to_apply=%region_50.51 | all-reduce | flops 1 | bytes 8 | tf_op jit(solution)/shard_map/psum | solution.py:111
  1513.0 62.7 %psum.77 = f32[]{:T(128)} all-reduce(f32[]{:T(128)} %multiply_reduce_fusion.6), channel_id=1, replica_groups=mesh['vox'=8,'fas'=16] {'vox','fas'}, use_global_device_ids=true, to_apply=%region_55.56 | all-reduce | flops 1 | bytes 8 | tf_op jit(solution)/shard_map/psum | solution.py:112
  1578.0 28.1 %while.220 = (s32[]{:T(128)}, f32[16,6144]{1,0:T(8,128)S(1)}, s32[]{:T(128)}, s32[256]{0:T(256)S(1)}, s32[]{:T(128)}, /*index=5*/bf16[256,64,64]{2,1,0:T(8,128)(...) while((s32[]{:T(128)}, f32[16,6144]{1,0:T(8,128)S(1)}, ...), condition=%wide.region_57.58_spmd.clone, body=%wide.region_56.57_spmd.clone.sunk | while | flops 1512153856 | bytes 31263864 | solution.py:68
  1606.9 69.0 %reduce-scatter.28.cloned.1.call-done = f32[16,384]{1,0:T(8,128)} async-done(((f32[16,6144]{1,0:T(8,128)}), f32[16,384]{1,0:T(8,128)}) %reduce-scatter.28.cloned.1.call-update) | async-done | bytes 24592 | tf_op jit(solution)/shard_map/reduce_scatter | solution.py:99
  1746.3 28.1 %while.222 = (s32[]{:T(128)}, f32[16,6144]{1,0:T(8,128)S(1)}, s32[]{:T(128)}, s32[256]{0:T(256)S(1)}, s32[]{:T(128)}, /*index=5*/bf16[256,64,64]{2,1,0:T(8,128)(...) while((s32[]{:T(128)}, f32[16,6144]{1,0:T(8,128)S(1)}, ...), condition=%wide.region_66.67_spmd.clone, body=%wide.region_65.66_spmd.clone.sunk | while | flops 1512153856 | bytes 31263864 | solution.py:68
  1775.2 71.6 %reduce-scatter.30.cloned.1.call-done = f32[16,384]{1,0:T(8,128)} async-done(((f32[16,6144]{1,0:T(8,128)}), f32[16,384]{1,0:T(8,128)}) %reduce-scatter.30.cloned.1.call-update) | async-done | bytes 24592 | tf_op jit(solution)/shard_map/reduce_scatter | solution.py:99
  1848.2 38.8 %psum.78 = f32[]{:T(128)} all-reduce(f32[]{:T(128)} %get-tuple-element.2540), channel_id=1, replica_groups=mesh['vox'=8,'fas'=16] {'fas'}, use_global_device_ids=true, to_apply=%region_64.65 | all-reduce | flops 1 | bytes 8 | tf_op jit(solution)/shard_map/psum | solution.py:111
  1887.0 62.8 %psum.79 = f32[]{:T(128)} all-reduce(f32[]{:T(128)} %multiply_reduce_fusion.5), channel_id=1, replica_groups=mesh['vox'=8,'fas'=16] {'vox','fas'}, use_global_device_ids=true, to_apply=%region_69.70 | all-reduce | flops 1 | bytes 8 | tf_op jit(solution)/shard_map/psum | solution.py:112
  1952.0 28.1 %while.223 = (s32[]{:T(128)}, f32[16,6144]{1,0:T(8,128)S(1)}, s32[]{:T(128)}, s32[256]{0:T(256)S(1)}, s32[]{:T(128)}, /*index=5*/bf16[256,64,64]{2,1,0:T(8,128)(...) while((s32[]{:T(128)}, f32[16,6144]{1,0:T(8,128)S(1)}, ...), condition=%wide.region_71.72_spmd.clone, body=%wide.region_70.71_spmd.clone.sunk | while | flops 1512153856 | bytes 31263864 | solution.py:68
  1980.9 69.1 %reduce-scatter.32.cloned.1.call-done = f32[16,384]{1,0:T(8,128)} async-done(((f32[16,6144]{1,0:T(8,128)}), f32[16,384]{1,0:T(8,128)}) %reduce-scatter.32.cloned.1.call-update) | async-done | bytes 24592 | tf_op jit(solution)/shard_map/reduce_scatter | solution.py:99
  (238 shorter events, 725.2 us)
Async XLA Ops:
  7.2 10.8 copy-start.15
  7.2 11.1 copy-start.14
  7.2 11.2 copy-start.16
  7.2 11.2 copy-start.11
  7.2 172.5 %reduce-scatter.12.cloned.1.call-start = ((), (), s32[]{:S(2)}) async-start(), calls=%async_computation.11 | async-start | bytes 417792 | tf_op jit(solution)/shard_map/reduce_scatter | solution.py:99
  18.5 58.1 %copy-start.17 = (s32[256]{0:T(256)S(1)}, s32[256]{0:T(256)}, u32[]{:S(2)}) copy-start(s32[256]{0:T(256)} %param.43) | copy-start | bytes 3076
  76.7 103.0 %copy-start.12 = (f32[16,384]{1,0:T(8,128)S(1)}, f32[16,384]{1,0:T(8,128)}, u32[]{:S(2)}) copy-start(f32[16,384]{1,0:T(8,128)} %param.40) | copy-start | bytes 73732
  104.6 0.7 copy-start.1
  105.4 141.2 %all-gather.11.cloned.1.call-start = ((), (), s32[]{:S(2)}) async-start(), calls=%async_computation.22 | async-start | bytes 1179648 | tf_op jit(solution)/shard_map/all_gather | solution.py:106
  224.5 126.1 %reduce-scatter.14.cloned.1.call-start = ((), (), s32[]{:S(2)}) async-start(), calls=%async_computation.12 | async-start | bytes 417792 | tf_op jit(solution)/shard_map/reduce_scatter | solution.py:99
  278.3 0.7 copy-start.2
  279.1 274.8 %reduce-scatter.16.cloned.1.call-start = ((), (), s32[]{:S(2)}) async-start(), calls=%async_computation.13 | async-start | bytes 417792 | tf_op jit(solution)/shard_map/reduce_scatter | solution.py:99
  484.0 0.7 copy-start.3
  484.8 135.9 %all-gather.13.cloned.1.call-start = ((), (), s32[]{:S(2)}) async-start(), calls=%async_computation.23 | async-start | bytes 1179648 | tf_op jit(solution)/shard_map/all_gather | solution.py:106
  598.6 126.1 %reduce-scatter.18.cloned.1.call-start = ((), (), s32[]{:S(2)}) async-start(), calls=%async_computation.14 | async-start | bytes 417792 | tf_op jit(solution)/shard_map/reduce_scatter | solution.py:99
  652.3 0.7 copy-start.4
  653.1 274.8 %reduce-scatter.20.cloned.1.call-start = ((), (), s32[]{:S(2)}) async-start(), calls=%async_computation.15 | async-start | bytes 417792 | tf_op jit(solution)/shard_map/reduce_scatter | solution.py:99
  858.0 0.7 copy-start.5
  858.8 135.9 %all-gather.15.cloned.1.call-start = ((), (), s32[]{:S(2)}) async-start(), calls=%async_computation.24 | async-start | bytes 1179648 | tf_op jit(solution)/shard_map/all_gather | solution.py:106
  972.6 126.2 %reduce-scatter.22.cloned.1.call-start = ((), (), s32[]{:S(2)}) async-start(), calls=%async_computation.16 | async-start | bytes 417792 | tf_op jit(solution)/shard_map/reduce_scatter | solution.py:99
  1026.3 0.7 copy-start.6
  1027.1 274.8 %reduce-scatter.24.cloned.1.call-start = ((), (), s32[]{:S(2)}) async-start(), calls=%async_computation.17 | async-start | bytes 417792 | tf_op jit(solution)/shard_map/reduce_scatter | solution.py:99
  1232.1 0.7 copy-start.7
  1232.8 135.9 %all-gather.17.cloned.1.call-start = ((), (), s32[]{:S(2)}) async-start(), calls=%async_computation.25 | async-start | bytes 1179648 | tf_op jit(solution)/shard_map/all_gather | solution.py:106
  1346.7 126.1 %reduce-scatter.26.cloned.1.call-start = ((), (), s32[]{:S(2)}) async-start(), calls=%async_computation.18 | async-start | bytes 417792 | tf_op jit(solution)/shard_map/reduce_scatter | solution.py:99
  1401.2 274.7 %reduce-scatter.28.cloned.1.call-start = ((), (), s32[]{:S(2)}) async-start(), calls=%async_computation.19 | async-start | bytes 417792 | tf_op jit(solution)/shard_map/reduce_scatter | solution.py:99
  1606.1 0.7 copy-start.9
  1606.9 135.9 %all-gather.19.cloned.1.call-start = ((), (), s32[]{:S(2)}) async-start(), calls=%async_computation.26 | async-start | bytes 1179648 | tf_op jit(solution)/shard_map/all_gather | solution.py:106
  1720.6 126.2 %reduce-scatter.30.cloned.1.call-start = ((), (), s32[]{:S(2)}) async-start(), calls=%async_computation.20 | async-start | bytes 417792 | tf_op jit(solution)/shard_map/reduce_scatter | solution.py:99
  1774.3 0.7 copy-start.10
  1775.1 274.9 %reduce-scatter.32.cloned.1.call-start = ((), (), s32[]{:S(2)}) async-start(), calls=%async_computation.21 | async-start | bytes 417792 | tf_op jit(solution)/shard_map/reduce_scatter | solution.py:99
  1951.1 0.9 copy-start.13
  (2 other events, 1.5 us)
Sparse Core Ops, SparseCore 0:
  105.5 74.1 reduce-scatter.11
  224.7 21.9 all-gather.10
  279.2 71.4 reduce-scatter.13
  484.9 68.9 reduce-scatter.15
  598.7 21.9 all-gather.12
  653.2 71.4 reduce-scatter.17
  858.9 68.9 reduce-scatter.19
  972.7 21.9 all-gather.14
  1027.2 71.5 reduce-scatter.21
  1233.0 68.9 reduce-scatter.23
  1346.8 21.9 all-gather.16
  1401.3 71.4 reduce-scatter.25
  1607.0 68.8 reduce-scatter.27
  1720.8 21.9 all-gather.18
  1775.2 71.5 reduce-scatter.29
  1981.0 68.9 reduce-scatter.31
